TPU v7x, 512 devices: a whole 4x4x16 slice. The times are simulated.
512 devices in a mesh: pb: 128 (over z, x, core), vert: 4 (over y).
Axes of the slice: x: 4, y: 4, z: 16, core: 2. Of those that a mesh axis runs over, the one named last changes fastest.
Arguments:
- orbitals: bfloat16 [256, 32, 1024], P('pb', None, 'vert'), may hold values from -6 to 6
- transition: float32 [256, 256], P('pb'), may hold values from -0.9 to 0.9
- trial: float32 [8, 256, 256], P('vert', 'pb'), may hold values from -6 to 6
- screened: bfloat16 [256, 1024, 1024], P('pb', None, 'vert'), may hold values from -0.00030517578 to 0.00030517578
- bare: bfloat16 [1024, 1024], replicated, may hold values from -6.1035156e-05 to 6.1035156e-05
- cheb: float32 [3], replicated, may hold values from 0.5 to 1.5
- pair_k: int32 [384], P('pb'), may hold values from 0 to 255
- pair_slot: int32 [384], P('pb'), may hold values from 0 to 1
- k_order: int32 [256], replicated, may hold values from 0 to 255, each once
Outputs:
- filtered: float32 [8, 256, 256], P('vert', 'pb')
Inputs may be any that keep to these rules, and one draw needn't show every extreme that they name: The pair i lies with the owner of its momentum transfer 2 * (i // 3) + pair_slot[i]. `k_order`: A permutation of the k-points.
All inputs are finite; a program needn't handle non-finite values.
Results may differ from a plain program's by a relative error of at most 0.0075.
Values may be sent and summed in bfloat16 or wider, within the bound.
No kernel may reach another device: no remote copies, remote signals or barrier semaphores. Data moves between devices by JAX's collectives and lax.ppermute only.
A program may use at most 64 MiB of HBM per device.

v0:
```python
import jax
import jax.numpy as jnp
from jax import lax
from jax.sharding import Mesh
from jax.sharding import PartitionSpec as P

NV = 16
PB = ("pb_0", "pb_1", "pb_2")


def laid_out(blocks, dim):
    shape = list(blocks.shape[1:])
    shape[dim] *= blocks.shape[0]
    return jnp.moveaxis(blocks, 0, dim).reshape(shape)


def gather_in_order(shard, axes, turns):
    blocks = shard[None]
    for k in turns:
        blocks = lax.all_gather(blocks, axes[k], axis=0, tiled=True)
    block = [lax.axis_size(axes[k]) for k in reversed(turns)]
    blocks = blocks.reshape(*block, *shard.shape)
    turned = sorted(range(len(turns)), key=lambda place: turns[len(turns) - 1 - place])
    return blocks.transpose(*turned, *range(len(turns), blocks.ndim)).reshape(-1, *shard.shape)


def gather_axes(shard, axes, turns, dim):
    return laid_out(gather_in_order(shard, axes, turns), dim)


def copy_for_each(shard, axis):
    count = lax.axis_size(axis)
    return lax.all_to_all(
        jnp.broadcast_to(shard[None], (count, *shard.shape)), axis, 0, 0, tiled=True
    )


def collect(shard, axis, dim):
    return laid_out(copy_for_each(shard, axis), dim)


def of_everyone(shard, axis):
    return copy_for_each(shard, axis).sum(axis=0)


def gather_axes_2(shard, axes, dim):
    far, near = axes
    blocks = copy_for_each(copy_for_each(shard, far), near)
    return laid_out(blocks.swapaxes(0, 1).reshape(-1, *shard.shape), dim)


def split_up(shard, dim, count):
    before, after = (shard.shape[:dim], shard.shape[dim + 1 :])
    return jnp.moveaxis(shard.reshape(*before, count, -1, *after), dim, 0)


def summed_on_arrival(shard, axis, dim):
    count = lax.axis_size(axis)
    blocks = lax.all_to_all(split_up(shard, dim, count), axis, 0, 0, tiled=True)
    return jnp.sum(blocks, axis=0)


def sum_in_two_steps(shard, axes, dim):
    far, near = axes
    blocks = split_up(shard, dim, lax.axis_size(far))
    nearer = summed_on_arrival(blocks, near, dim + 1)
    arrived = lax.all_to_all(nearer, far, split_axis=0, concat_axis=0, tiled=True)
    return arrived.sum(axis=0)


def by_axis(shard, axes):
    far, near = axes
    nearer = of_everyone(shard, near)
    return of_everyone(nearer, far)


def body(orbitals, transition, trial, screened, bare, cheb, pair_k, pair_slot, k_order):
    kpoint_local = orbitals.shape[0]
    band_all = orbitals.shape[1]
    point_local = orbitals.shape[2]
    pair_count = pair_k.shape[0]
    kpoint_total = k_order.shape[0]
    valence = NV
    conduction = band_all - valence
    pair_width = valence * conduction
    end_count = 2 * pair_count
    hp = lax.Precision.HIGHEST
    position = lax.axis_index(PB)
    momentum = position * kpoint_local + pair_slot
    partner = jnp.mod(pair_k - momentum, kpoint_total)
    pair_ends = jnp.stack([pair_k, partner], axis=1).reshape(-1)
    owner_rows = jnp.arange(kpoint_total, dtype=jnp.int32)
    destination = jnp.sum(
        jnp.where(pair_ends[:, None] == k_order[None, :], owner_rows[None, :], 0), axis=1
    )
    shard_piece = gather_axes(orbitals, PB, (1, 0, 2), 0)
    row_count = shard_piece.shape[0]
    onehot = (destination[:, None] == jnp.arange(row_count, dtype=jnp.int32)[None, :]).astype(
        jnp.bfloat16
    )
    picked = jnp.dot(onehot, shard_piece.reshape(row_count, -1), preferred_element_type=jnp.float32)
    picked = picked.astype(jnp.bfloat16).reshape(end_count, band_all, point_local)
    val_points = collect(picked[:, :valence, :], "vert", 2)
    point_total = val_points.shape[2]
    val_pairs = val_points.reshape(pair_count, 2, valence, point_total)
    cond_pairs = picked[:, valence:, :].reshape(pair_count, 2, conduction, point_local)

    def build_block(pair_index):
        val_both = val_pairs[pair_index].astype(jnp.float32)
        cond_both = cond_pairs[pair_index].astype(jnp.float32)
        left_pair = (
            (val_both[0][:, None, :] * val_both[1][None, :, :])
            .reshape(valence * valence, point_total)
            .astype(jnp.bfloat16)
        )
        right_pair = (
            (cond_both[0][:, None, :] * cond_both[1][None, :, :])
            .reshape(conduction * conduction, point_local)
            .astype(jnp.bfloat16)
        )
        matrix = screened[pair_slot[pair_index]]
        half_product = jnp.dot(left_pair, matrix, preferred_element_type=jnp.float32).astype(
            jnp.bfloat16
        )
        block_part = lax.dot_general(
            half_product, right_pair, (((1,), (1,)), ((), ())), preferred_element_type=jnp.float32
        )
        return (
            block_part.reshape(valence, valence, conduction, conduction)
            .transpose(0, 2, 1, 3)
            .reshape(pair_width, pair_width)
        )

    block_parts = lax.map(build_block, jnp.arange(pair_count, dtype=jnp.int32))
    blocks = of_everyone(block_parts, "vert")
    gathered_own = collect(orbitals, "vert", 2).astype(jnp.float32)
    products = (
        (gathered_own[:, :valence, None, :] * gathered_own[:, None, valence:, :])
        .reshape(kpoint_local, pair_width, point_total)
        .astype(jnp.bfloat16)
    )

    def pick_trial(shard_piece):
        row_count = shard_piece.shape[1]
        onehot = (destination[:, None] == jnp.arange(row_count, dtype=jnp.int32)[None, :]).astype(
            jnp.bfloat16
        )
        return jnp.einsum("er,nrj->nej", onehot, shard_piece, preferred_element_type=jnp.float32)

    def apply_kernel(current):
        fetched = pick_trial(gather_axes_2(current, (("pb_0", "pb_1"), "pb_2"), 1)).astype(
            jnp.bfloat16
        )
        pair_view = fetched.astype(jnp.float32).reshape(fetched.shape[0], pair_count, 2, pair_width)
        toward_first = jnp.einsum("pij,npj->npi", blocks, pair_view[:, :, 1], precision=hp)
        toward_second = jnp.einsum("pij,npi->npj", blocks, pair_view[:, :, 0], precision=hp)
        results = jnp.stack([toward_first, toward_second], axis=2).reshape(
            fetched.shape[0], end_count, pair_width
        )
        onehot = (
            jnp.arange(kpoint_local * lax.axis_size(PB), dtype=jnp.int32)[:, None]
            == destination[None, :]
        ).astype(jnp.float32)
        screened_term = sum_in_two_steps(
            jnp.einsum("re,nej->rnj", onehot, results, precision=hp), (("pb_0", "pb_1"), "pb_2"), 0
        ).transpose(1, 0, 2)
        partial_density = jnp.einsum(
            "nkj,kjm->nm", current, products, preferred_element_type=jnp.float32
        )
        density = by_axis(partial_density, (("pb_0", "pb_1"), "pb_2")).astype(jnp.bfloat16)
        potential = jnp.einsum(
            "nv,mv->nm", density, bare, preferred_element_type=jnp.float32
        ).astype(jnp.bfloat16)
        bare_term = jnp.einsum(
            "kjm,nm->nkj", products, potential, preferred_element_type=jnp.float32
        )
        return transition[None] * current.astype(jnp.float32) + 2.0 * bare_term - screened_term

    first_step = apply_kernel(trial.astype(jnp.bfloat16))
    second_step = 2.0 * apply_kernel(first_step.astype(jnp.bfloat16)) - trial
    return cheb[0] * trial + cheb[1] * first_step + cheb[2] * second_step


def solution(mesh):
    split = Mesh(
        mesh.devices.reshape(16, 4, 2, mesh.shape["vert"]), ("pb_0", "pb_1", "pb_2", "vert")
    )
    in_specs = (
        P(PB, None, "vert"),
        P(PB, None),
        P("vert", PB, None),
        P(PB, None, "vert"),
        P(),
        P(),
        P(PB),
        P(PB),
        P(),
    )
    out_specs = P("vert", PB, None)
    return jax.shard_map(body, mesh=split, in_specs=in_specs, out_specs=out_specs, check_vma=False)
```

profile of v0, /device:TPU:2, one launch (start us, length us, event | category | flops | bytes accessed | tf_op | source)
XLA Modules:
  0.0 449.6 jit_solution(13693576423494758041)
XLA Ops:
  6.6 17.1 %all-gather = bf16[8,32,256]{2,1,0:T(8,128)(2,1)} all-gather(bf16[2,32,256]{2,1,0:T(8,128)(2,1)} %param.11), channel_id=2, replica_groups=mesh['pb_0'=16,'pb_1'=4,'pb_2'=2,'vert'=4] {'pb_1'}, dimensions={0}, use_global_device_ids=true | all-gather | bytes 163840 | tf_op jit(solution)/shard_map/all_gather | solution.py:20
  23.8 72.9 %all-gather.4.cloned.1.call-done = bf16[64,2,32,256]{3,2,1,0:T(8,128)(2,1)} async-done(((bf16[4,2,32,256]{3,2,1,0:T(8,128)(2,1)}), bf16[64,2,32,256]{3,2,1,0:T(8,128)(2,1)}) %all-gather.4.cloned.1.call-update) | async-done | bytes 2097168 | tf_op jit(solution)/shard_map/all_gather | solution.py:20
  97.4 4.3 all-to-all-start
  102.1 5.5 %all-to-all-done = bf16[4,2,32,256]{3,2,1,0:T(8,128)(2,1)S(1)} async-done(((bf16[4,2,32,256]{3,2,1,0:T(8,128)(2,1)}), bf16[4,2,32,256]{3,2,1,0:T(8,128)(2,1)S(1)}, u32[]{:S(2)}, u32[]{:S(2)}) %all-to-all-start) | async-done | bytes 131104 | tf_op jit(solution)/shard_map/all_to_all | solution.py:33
  108.3 11.3 %all-to-all-start.3 = ((bf16[64,2,2,256]{3,2,1,0:T(2,128)(2,1)}), bf16[64,2,2,256]{3,2,1,0:T(2,128)(2,1)S(1)}, u32[]{:S(2)}, u32[]{:S(2)}) async-start(bf16[64,2,2,256]{3,2,1,0:T(2,128)(2,1)} %broadcast_in_dim.50), calls=%async_computation.3 | async-start | bytes 262144 | tf_op jit(solution)/shard_map/all_to_all | solution.py:33
  119.9 2.6 copy.171
  122.5 4.3 copy.205
  128.2 6.5 %all-to-all-done.3 = bf16[64,2,2,256]{3,2,1,0:T(2,128)(2,1)S(1)} async-done(((bf16[64,2,2,256]{3,2,1,0:T(2,128)(2,1)}), bf16[64,2,2,256]{3,2,1,0:T(2,128)(2,1)S(1)}, u32[]{:S(2)}, u32[]{:S(2)}) %all-to-all-start.3) | async-done | bytes 131104 | tf_op jit(solution)/shard_map/all_to_all | solution.py:33
  135.4 3.4 all-to-all-start.5
  139.8 5.3 %all-to-all-done.5 = bf16[4,6,16,256]{3,2,1,0:T(8,128)(2,1)S(1)} async-done(((bf16[4,6,16,256]{3,2,1,0:T(8,128)(2,1)}), bf16[4,6,16,256]{3,2,1,0:T(8,128)(2,1)S(1)}, u32[]{:S(2)}, u32[]{:S(2)}) %all-to-all-start.5) | async-done | bytes 196640 | tf_op jit(solution)/shard_map/all_to_all | solution.py:33
  145.7 3.2 all-to-all-start.1
  150.5 43.2 %while.10 = (s32[]{:T(128)}, f32[3,256,256]{2,1,0:T(8,128)}, s32[3]{0:T(128)}, bf16[3,2,16,1024]{3,2,1,0:T(8,128)(2,1)}, s32[3]{0:T(128)}, /*index=5*/bf16[2,102...) while((s32[]{:T(128)}, f32[3,256,256]{2,1,0:T(8,128)}, ...), condition=%wide.region_4.5_spmd, body=%wide.region_3.4_spmd.sunk | while | flops 168534016 | bytes 3883733 | solution.py:134
  193.8 3.9 all_to_all.75
  197.7 3.1 broadcast_in_dim.55
  200.8 5.0 %all-to-all-start.6 = ((f32[4,3,256,256]{3,2,1,0:T(8,128)}), f32[4,3,256,256]{3,2,1,0:T(8,128)}, u32[]{:S(2)}, u32[]{:S(2)}) async-start(f32[4,3,256,256]{3,2,1,0:T(8,128)} %broadcast_in_dim.55), calls=%async_computation.6 | async-start | bytes 6291456 | tf_op jit(solution)/shard_map/all_to_all | solution.py:33
  208.2 35.7 %all-to-all-done.6 = f32[4,3,256,256]{3,2,1,0:T(8,128)} async-done(((f32[4,3,256,256]{3,2,1,0:T(8,128)}), f32[4,3,256,256]{3,2,1,0:T(8,128)}, u32[]{:S(2)}, u32[]{:S(2)}) %all-to-all-start.6) | async-done | bytes 3145760 | tf_op jit(solution)/shard_map/all_to_all | solution.py:33
  243.8 3.1 reduce_sum.93
  250.6 4.9 %all_to_all.76 = f32[2,64,2,2,256]{4,1,3,2,0:T(8,128)} all-to-all(f32[2,64,2,2,256]{4,1,3,2,0:T(8,128)S(1)} %convolution_bitcast_fusion.2), channel_id=1, replica_groups=mesh['pb_0'=16,'pb_1'=4,'pb_2'=2,'vert'=4] {'pb_2'}, dimensions={0} | all-to-all | bytes 1048576 | tf_op jit(solution)/shard_map/all_to_all | solution.py:59
  256.4 10.3 %all-to-all-start.2 = ((f32[64,2,1024]{2,1,0:T(2,128)}), f32[64,2,1024]{2,1,0:T(2,128)}, u32[]{:S(2)}, u32[]{:S(2)}) async-start(f32[64,2,1024]{2,1,0:T(2,128)} %broadcast_in_dim.46), calls=%async_computation.2 | async-start | bytes 1048576 | tf_op jit(solution)/shard_map/all_to_all | solution.py:33
  268.8 30.9 %all-to-all-done.2 = f32[64,2,1024]{2,1,0:T(2,128)} async-done(((f32[64,2,1024]{2,1,0:T(2,128)}), f32[64,2,1024]{2,1,0:T(2,128)}, u32[]{:S(2)}, u32[]{:S(2)}) %all-to-all-start.2) | async-done | bytes 524320 | tf_op jit(solution)/shard_map/all_to_all | solution.py:33
  299.7 6.0 %all-to-all-start.8 = ((f32[64,2,2,256]{3,2,1,0:T(2,128)}), f32[64,2,2,256]{3,2,1,0:T(2,128)S(1)}, u32[]{:S(2)}, u32[]{:S(2)}) async-start(f32[64,2,2,256]{3,2,1,0:T(2,128)} %copy.176), calls=%async_computation.8 | async-start | bytes 524288 | tf_op jit(solution)/shard_map/all_to_all | solution.py:67
  306.8 19.9 %all-to-all-done.8 = f32[64,2,2,256]{3,2,1,0:T(2,128)S(1)} async-done(((f32[64,2,2,256]{3,2,1,0:T(2,128)}), f32[64,2,2,256]{3,2,1,0:T(2,128)S(1)}, u32[]{:S(2)}, u32[]{:S(2)}) %all-to-all-start.8) | async-done | bytes 262176 | tf_op jit(solution)/shard_map/all_to_all | solution.py:67
  328.6 5.8 %all-to-all-start.11 = ((bf16[64,2,2,256]{3,2,1,0:T(2,128)(2,1)}), bf16[64,2,2,256]{3,2,1,0:T(2,128)(2,1)S(1)}, u32[]{:S(2)}, u32[]{:S(2)}) async-start(bf16[64,2,2,256]{3,2,1,0:T(2,128)(2,1)} %broadcast_in_dim.58), calls=%async_computation.11 | async-start | bytes 262144 | tf_op jit(solution)/shard_map/all_to_all | solution.py:33
  334.6 15.3 %all-to-all-done.11 = bf16[64,2,2,256]{3,2,1,0:T(2,128)(2,1)S(1)} async-done(((bf16[64,2,2,256]{3,2,1,0:T(2,128)(2,1)}), bf16[64,2,2,256]{3,2,1,0:T(2,128)(2,1)S(1)}, u32[]{:S(2)}, u32[]{:S(2)}) %all-to-all-start.11) | async-done | bytes 131104 | tf_op jit(solution)/shard_map/all_to_all | solution.py:33
  350.2 3.9 all_to_all.77
  360.1 4.9 %all_to_all.78 = f32[2,64,2,2,256]{4,1,3,2,0:T(8,128)} all-to-all(f32[2,64,2,2,256]{4,1,3,2,0:T(8,128)S(1)} %convolution_bitcast_fusion.1), channel_id=1, replica_groups=mesh['pb_0'=16,'pb_1'=4,'pb_2'=2,'vert'=4] {'pb_2'}, dimensions={0} | all-to-all | bytes 1048576 | tf_op jit(solution)/shard_map/all_to_all | solution.py:59
  365.6 3.2 all-to-all-start.9
  370.8 5.4 %all-to-all-start.14 = ((f32[64,2,2,256]{3,2,1,0:T(2,128)}), f32[64,2,2,256]{3,2,1,0:T(2,128)S(1)}, u32[]{:S(2)}, u32[]{:S(2)}) async-start(f32[64,2,2,256]{3,2,1,0:T(2,128)} %copy.187), calls=%async_computation.14 | async-start | bytes 524288 | tf_op jit(solution)/shard_map/all_to_all | solution.py:67
  376.3 22.5 %all-to-all-done.14 = f32[64,2,2,256]{3,2,1,0:T(2,128)S(1)} async-done(((f32[64,2,2,256]{3,2,1,0:T(2,128)}), f32[64,2,2,256]{3,2,1,0:T(2,128)S(1)}, u32[]{:S(2)}, u32[]{:S(2)}) %all-to-all-start.14) | async-done | bytes 262176 | tf_op jit(solution)/shard_map/all_to_all | solution.py:67
  399.7 6.2 %all-to-all-start.10 = ((f32[64,2,1024]{2,1,0:T(2,128)}), f32[64,2,1024]{2,1,0:T(2,128)}, u32[]{:S(2)}, u32[]{:S(2)}) async-start(f32[64,2,1024]{2,1,0:T(2,128)} %broadcast_in_dim.57), calls=%async_computation.10 | async-start | bytes 1048576 | tf_op jit(solution)/shard_map/all_to_all | solution.py:33
  406.7 31.5 %all-to-all-done.10 = f32[64,2,1024]{2,1,0:T(2,128)} async-done(((f32[64,2,1024]{2,1,0:T(2,128)}), f32[64,2,1024]{2,1,0:T(2,128)}, u32[]{:S(2)}, u32[]{:S(2)}) %all-to-all-start.10) | async-done | bytes 524320 | tf_op jit(solution)/shard_map/all_to_all | solution.py:33
  439.3 2.8 fusion.16
  (135 shorter events, 63.6 us)
Async XLA Ops:
  6.5 320.4 %copy-start = (bf16[1024,1024]{1,0:T(8,128)(2,1)S(1)}, bf16[1024,1024]{1,0:T(8,128)(2,1)}, u32[]{:S(2)}) copy-start(bf16[1024,1024]{1,0:T(8,128)(2,1)} %param.15) | copy-start | bytes 6291460
  6.5 90.2 %copy-start.2 = (bf16[2,32,256]{2,1,0:T(8,128)(2,1)S(1)}, bf16[2,32,256]{2,1,0:T(8,128)(2,1)}, u32[]{:S(2)}) copy-start(bf16[2,32,256]{2,1,0:T(8,128)(2,1)} %param.11) | copy-start | bytes 98308
  6.5 95.1 %copy-start.11 = (s32[3]{0:T(128)S(1)}, s32[3]{0:T(128)}, u32[]{:S(2)}) copy-start(s32[3]{0:T(128)} %param.17) | copy-start | bytes 40
  6.5 95.1 %copy-start.13 = (s32[3]{0:T(128)S(1)}, s32[3]{0:T(128)}, u32[]{:S(2)}) copy-start(s32[3]{0:T(128)} %param.18) | copy-start | bytes 40
  6.5 95.3 %copy-start.5 = (f32[2,2,256]{2,1,0:T(2,128)S(1)}, f32[2,2,256]{2,1,0:T(2,128)}, u32[]{:S(2)}) copy-start(f32[2,2,256]{2,1,0:T(2,128)} %param.13) | copy-start | bytes 12292
  6.6 95.3 %copy-start.12 = (s32[256]{0:T(256)S(1)}, s32[256]{0:T(256)}, u32[]{:S(2)}) copy-start(s32[256]{0:T(256)} %param.19) | copy-start | bytes 3076
  6.6 90.1 %all-gather.4.cloned.1.call-start = ((), (), s32[]{:S(2)}) async-start(), calls=%async_computation.15 | async-start | bytes 2228224 | tf_op jit(solution)/shard_map/all_gather | solution.py:20
  23.7 96.2 %all-gather.6.cloned.1.call-start = ((), (), s32[]{:S(2)}) async-start(), calls=%async_computation.16 | async-start | bytes 6291456 | tf_op jit(solution)/shard_map/all_gather | solution.py:20
  97.4 10.3 %all-to-all-start = ((bf16[4,2,32,256]{3,2,1,0:T(8,128)(2,1)}), bf16[4,2,32,256]{3,2,1,0:T(8,128)(2,1)S(1)}, u32[]{:S(2)}, u32[]{:S(2)}) async-start(bf16[4,2,32,256]{3,2,1,0:T(8,128)(2,1)} %broadcast_in_dim.44), calls=%async_computation | async-start | bytes 262144 | tf_op jit(solution)/shard_map/all_to_all | solution.py:33
  101.9 36.9 %copy-start.3 = (bf16[2,2,256]{2,0,1:T(2,128)(2,1)}, bf16[2,2,256]{2,0,1:T(2,128)(2,1)S(1)}, u32[]{:S(2)}) copy-start(bf16[2,2,256]{2,0,1:T(2,128)(2,1)S(1)} %copy.214) | copy-start | bytes 6148
  102.1 24.8 %copy-start.7 = (s32[6]{0:T(128)}, s32[6]{0:T(128)S(1)}, u32[]{:S(2)}) copy-start(s32[6]{0:T(128)S(1)} %select_reduce_fusion) | copy-start | bytes 76
  108.3 26.4 %all-to-all-start.3 = ((bf16[64,2,2,256]{3,2,1,0:T(2,128)(2,1)}), bf16[64,2,2,256]{3,2,1,0:T(2,128)(2,1)S(1)}, u32[]{:S(2)}, u32[]{:S(2)}) async-start(bf16[64,2,2,256]{3,2,1,0:T(2,128)(2,1)} %broadcast_in_dim.50), calls=%async_computation.3 | async-start | bytes 262144 | tf_op jit(solution)/shard_map/all_to_all | solution.py:33
  135.4 9.7 %all-to-all-start.5 = ((bf16[4,6,16,256]{3,2,1,0:T(8,128)(2,1)}), bf16[4,6,16,256]{3,2,1,0:T(8,128)(2,1)S(1)}, u32[]{:S(2)}, u32[]{:S(2)}) async-start(bf16[4,6,16,256]{3,2,1,0:T(8,128)(2,1)} %broadcast_in_dim.54), calls=%async_computation.5 | async-start | bytes 393216 | tf_op jit(solution)/shard_map/all_to_all | solution.py:33
  145.7 47.9 %all-to-all-start.1 = ((f32[2,2,1024]{2,1,0:T(2,128)}), f32[2,2,1024]{2,1,0:T(2,128)S(1)}, u32[]{:S(2)}, u32[]{:S(2)}) async-start(f32[2,2,1024]{2,1,0:T(2,128)} %broadcast_in_dim.45), calls=%async_computation.1 | async-start | bytes 32768 | tf_op jit(solution)/shard_map/all_to_all | solution.py:33
  150.5 43.2 %copy-start.1 = (bf16[64,2,2,256]{3,2,0,1:T(2,128)(2,1)S(1)}, bf16[64,2,2,256]{3,2,0,1:T(2,128)(2,1)}, u32[]{:S(2)}) copy-start(bf16[64,2,2,256]{3,2,0,1:T(2,128)(2,1)} %copy.166) | copy-start | bytes 393220
  200.8 6.2 %copy-start.8 = (s32[6]{0:T(128)S(1)}, s32[6]{0:T(128)}, u32[]{:S(2)}) copy-start(s32[6]{0:T(128)} %copy-done.7) | copy-start | bytes 76
  200.8 43.0 %all-to-all-start.6 = ((f32[4,3,256,256]{3,2,1,0:T(8,128)}), f32[4,3,256,256]{3,2,1,0:T(8,128)}, u32[]{:S(2)}, u32[]{:S(2)}) async-start(f32[4,3,256,256]{3,2,1,0:T(8,128)} %broadcast_in_dim.55), calls=%async_computation.6 | async-start | bytes 6291456 | tf_op jit(solution)/shard_map/all_to_all | solution.py:33
  255.5 71.4 %copy-start.4 = (bf16[2,2,256]{2,0,1:T(2,128)(2,1)S(1)}, bf16[2,2,256]{2,0,1:T(2,128)(2,1)}, u32[]{:S(2)}) copy-start(bf16[2,2,256]{2,0,1:T(2,128)(2,1)} %copy-done.3) | copy-start | bytes 6148
  255.5 71.4 %copy-start.9 = (f32[2,256]{1,0:T(2,128)S(1)}, f32[2,256]{1,0:T(2,128)}, u32[]{:S(2)}) copy-start(f32[2,256]{1,0:T(2,128)} %param.12) | copy-start | bytes 6148
  256.4 43.2 %all-to-all-start.2 = ((f32[64,2,1024]{2,1,0:T(2,128)}), f32[64,2,1024]{2,1,0:T(2,128)}, u32[]{:S(2)}, u32[]{:S(2)}) async-start(f32[64,2,1024]{2,1,0:T(2,128)} %broadcast_in_dim.46), calls=%async_computation.2 | async-start | bytes 1048576 | tf_op jit(solution)/shard_map/all_to_all | solution.py:33
  299.7 27.1 %all-to-all-start.8 = ((f32[64,2,2,256]{3,2,1,0:T(2,128)}), f32[64,2,2,256]{3,2,1,0:T(2,128)S(1)}, u32[]{:S(2)}, u32[]{:S(2)}) async-start(f32[64,2,2,256]{3,2,1,0:T(2,128)} %copy.176), calls=%async_computation.8 | async-start | bytes 524288 | tf_op jit(solution)/shard_map/all_to_all | solution.py:67
  328.6 21.3 %all-to-all-start.11 = ((bf16[64,2,2,256]{3,2,1,0:T(2,128)(2,1)}), bf16[64,2,2,256]{3,2,1,0:T(2,128)(2,1)S(1)}, u32[]{:S(2)}, u32[]{:S(2)}) async-start(bf16[64,2,2,256]{3,2,1,0:T(2,128)(2,1)} %broadcast_in_dim.58), calls=%async_computation.11 | async-start | bytes 262144 | tf_op jit(solution)/shard_map/all_to_all | solution.py:33
  360.1 45.8 %copy-start.10 = (f32[3]{0:T(128)S(1)}, f32[3]{0:T(128)}, u32[]{:S(2)}) copy-start(f32[3]{0:T(128)} %param.16) | copy-start | bytes 40
  365.6 5.3 %all-to-all-start.9 = ((f32[2,2,1024]{2,1,0:T(2,128)}), f32[2,2,1024]{2,1,0:T(2,128)S(1)}, u32[]{:S(2)}, u32[]{:S(2)}) async-start(f32[2,2,1024]{2,1,0:T(2,128)} %broadcast_in_dim.56), calls=%async_computation.9 | async-start | bytes 32768 | tf_op jit(solution)/shard_map/all_to_all | solution.py:33
  368.8 70.5 %copy-start.6 = (f32[2,2,256]{2,1,0:T(2,128)S(1)}, f32[2,2,256]{2,1,0:T(2,128)}, u32[]{:S(2)}) copy-start(f32[2,2,256]{2,1,0:T(2,128)} %param.13) | copy-start | bytes 12292
  370.8 27.9 %all-to-all-start.14 = ((f32[64,2,2,256]{3,2,1,0:T(2,128)}), f32[64,2,2,256]{3,2,1,0:T(2,128)S(1)}, u32[]{:S(2)}, u32[]{:S(2)}) async-start(f32[64,2,2,256]{3,2,1,0:T(2,128)} %copy.187), calls=%async_computation.14 | async-start | bytes 524288 | tf_op jit(solution)/shard_map/all_to_all | solution.py:67
  399.7 38.4 %all-to-all-start.10 = ((f32[64,2,1024]{2,1,0:T(2,128)}), f32[64,2,1024]{2,1,0:T(2,128)}, u32[]{:S(2)}, u32[]{:S(2)}) async-start(f32[64,2,1024]{2,1,0:T(2,128)} %broadcast_in_dim.57), calls=%async_computation.10 | async-start | bytes 1048576 | tf_op jit(solution)/shard_map/all_to_all | solution.py:33
Sparse Core Ops, SparseCore 0:
  23.8 72.7 all-gather.3
  98.8 21.0 all-gather.5
where the time goes:
time: 452 us; the launch traced here: 450 us
  waiting for transfers between devices  246 us (54%)
  starting transfers between devices  64 us (14%)
  local copies, waits for them, and re-layouts  42.1 us (9%)
  blocking collectives  34.8 us (8%)
  matrix products  23.8 us (5%)
  between operations  13.8 us (3%)
  other arithmetic  13.4 us (3%)
  loops' own time  11.5 us (3%)
    all_to_all x9, waiting for transfers between devices, copy_for_each(): lax.all_to_all(jnp.broadcast_to(shard[None], (count, *shard.shape)), axis...  131 us
    all_gather x2, waiting for transfers between devices, gather_in_order(): blocks = lax.all_gather(blocks, axes[k], axis=0, tiled=True)  72.9 us
    all_to_all x9, starting transfers between devices, copy_for_each(): lax.all_to_all(jnp.broadcast_to(shard[None], (count, *shard.shape)), axis...  52.6 us
    all_to_all x2, waiting for transfers between devices, sum_in_two_steps(): lax.all_to_all(nearer, far, split_axis=0, concat_axis=0, tiled=True)  42.4 us
    all_gather x1, blocking collectives, gather_in_order(): blocks = lax.all_gather(blocks, axes[k], axis=0, tiled=True)  17.1 us
    another operation x1, loops' own time, body(): block_parts = lax.map(build_block, jnp.arange(pair_count, dtype=jnp.int32))  11.5 us
    all_to_all x2, starting transfers between devices, sum_in_two_steps(): lax.all_to_all(nearer, far, split_axis=0, concat_axis=0, tiled=True)  11.4 us
    all_to_all x2, blocking collectives, summed_on_arrival(): blocks = lax.all_to_all(split_up(shard, dim, count), axis, 0, 0, tiled=True)  9.81 us
  transfers between devices with their start and end apart: 13, of which 10 were waited for; matrix products, arithmetic and copies ran while one was open for 12% of the time, Pallas kernels for 0%

commit v1 on v0

--- a/solution.py
+++ b/solution.py
@@ -17,7 +17,9 @@
 def gather_in_order(shard, axes, turns):
     blocks = shard[None]
     for k in turns:
-        blocks = lax.all_gather(blocks, axes[k], axis=0, tiled=True)
+        blocks = jnp.concatenate(
+            lax.all_to_all(jnp.stack([blocks] * lax.axis_size(axes[k])), axes[k], 0, 0), axis=0
+        )
     block = [lax.axis_size(axes[k]) for k in reversed(turns)]
     blocks = blocks.reshape(*block, *shard.shape)
     turned = sorted(range(len(turns)), key=lambda place: turns[len(turns) - 1 - place])

time: 452 us -> 476 us (1.053)
  between operations: 13.8 us -> 0.45 us
  waiting for transfers between devices: 246 us -> 259 us
  blocking collectives: 34.8 us -> 47 us
  starting transfers between devices: 64 us -> 71.4 us
    all_to_all x0 -> x1, waiting for transfers between devices: none -> 88.8 us  [gather_in_order(): lax.all_to_all(jnp.stack([blocks] * lax.axis_size(axes[k])), axes[k], 0, 0)]
    all_gather x2 -> x0, waiting for transfers between devices: 72.9 us -> none  [gather_in_order(): blocks = lax.all_gather(blocks, axes[k], axis=0, tiled=True)]
    all_to_all x0 -> x2, blocking collectives: none -> 20.9 us  [gather_in_order(): lax.all_to_all(jnp.stack([blocks] * lax.axis_size(axes[k])), axes[k], 0, 0)]
    all_gather x1 -> x0, blocking collectives: 17.1 us -> none  [gather_in_order(): blocks = lax.all_gather(blocks, axes[k], axis=0, tiled=True)]
    all_to_all x0 -> x1, starting transfers between devices: none -> 13.6 us  [gather_in_order(): lax.all_to_all(jnp.stack([blocks] * lax.axis_size(axes[k])), axes[k], 0, 0)]
    all_to_all x2 -> x3, blocking collectives: 7.89 us -> 16.2 us  [copy_for_each(): lax.all_to_all(jnp.broadcast_to(shard[None], (count, *shard.shape)), axis...]
    all_to_all x9 -> x8, starting transfers between devices: 52.6 us -> 46.4 us  [copy_for_each(): lax.all_to_all(jnp.broadcast_to(shard[None], (count, *shard.shape)), axis...]
    another operation x0 -> x3, local copies, waits for them, and re-layouts: none -> 5.18 us  [the longest x1 2.63 us: gather_in_order(): blocks = blocks.reshape(*block, *shard.shape)]
  transfers between devices with their start and end apart: 13 -> 11, of which waited for: 10 -> 9; matrix products, arithmetic and copies ran while one was open for 12% -> 11% of each run, Pallas kernels for 0% -> 0%
where the time goes in v1:
time: 476 us; the launch traced here: 473 us
  waiting for transfers between devices  259 us (54%)
  starting transfers between devices  71.4 us (15%)
  blocking collectives  47 us (10%)
  local copies, waits for them, and re-layouts  44.7 us (9%)
  matrix products  23.7 us (5%)
  other arithmetic  16 us (3%)
  loops' own time  11.5 us (2%)
    all_to_all x8, waiting for transfers between devices, copy_for_each(): lax.all_to_all(jnp.broadcast_to(shard[None], (count, *shard.shape)), axis...  127 us
    all_to_all x1, waiting for transfers between devices, gather_in_order(): lax.all_to_all(jnp.stack([blocks] * lax.axis_size(axes[k])), axes[k], 0, 0)  88.8 us
    all_to_all x8, starting transfers between devices, copy_for_each(): lax.all_to_all(jnp.broadcast_to(shard[None], (count, *shard.shape)), axis...  46.4 us
    all_to_all x2, waiting for transfers between devices, sum_in_two_steps(): lax.all_to_all(nearer, far, split_axis=0, concat_axis=0, tiled=True)  42.4 us
    all_to_all x2, blocking collectives, gather_in_order(): lax.all_to_all(jnp.stack([blocks] * lax.axis_size(axes[k])), axes[k], 0, 0)  20.9 us
    all_to_all x3, blocking collectives, copy_for_each(): lax.all_to_all(jnp.broadcast_to(shard[None], (count, *shard.shape)), axis...  16.2 us
    all_to_all x1, starting transfers between devices, gather_in_order(): lax.all_to_all(jnp.stack([blocks] * lax.axis_size(axes[k])), axes[k], 0, 0)  13.6 us
    another operation x1, loops' own time, body(): block_parts = lax.map(build_block, jnp.arange(pair_count, dtype=jnp.int32))  11.5 us
  transfers between devices with their start and end apart: 11, of which 9 were waited for; matrix products, arithmetic and copies ran while one was open for 11% of the time, Pallas kernels for 0%

profile of v1, /device:TPU:2, one launch (start us, length us, event | category | flops | bytes accessed | tf_op | source)
XLA Modules:
  0.0 473.4 jit_solution(6426322477262596874)
XLA Ops:
  0.9 12.8 %all_to_all.90 = bf16[4,1,2,32,256]{4,3,2,1,0:T(8,128)(2,1)S(1)} all-to-all(bf16[4,1,2,32,256]{4,3,2,1,0:T(8,128)(2,1)S(1)} %stack.39), channel_id=1, replica_groups=mesh['pb_0'=16,'pb_1'=4,'pb_2'=2,'vert'=4] {'pb_1'}, dimensions={0} | all-to-all | bytes 262144 | tf_op jit(solution)/shard_map/all_to_all | solution.py:21
  14.5 8.4 %all_to_all.91 = bf16[4,2,32,256]{3,2,1,0:T(8,128)(2,1)S(1)} all-to-all(bf16[4,2,32,256]{3,2,1,0:T(8,128)(2,1)S(1)} %broadcast_in_dim.42), channel_id=1, replica_groups=mesh['pb_0'=16,'pb_1'=4,'pb_2'=2,'vert'=4] {'vert'}, dimensions={0} | all-to-all | bytes 262144 | tf_op jit(solution)/shard_map/all_to_all | solution.py:35
  24.5 13.6 %all-to-all-start.6 = ((bf16[16,4,2,32,256]{4,3,2,1,0:T(8,128)(2,1)}), bf16[16,4,2,32,256]{4,3,2,1,0:T(8,128)(2,1)}, u32[]{:S(2)}, u32[]{:S(2)}) async-start(bf16[16,4,2,32,256]{4,3,2,1,0:T(8,128)(2,1)} %stack.40), calls=%async_computation.6 | async-start | bytes 4194304 | tf_op jit(solution)/shard_map/all_to_all | solution.py:21
  38.9 88.8 %all-to-all-done.6 = bf16[16,4,2,32,256]{4,3,2,1,0:T(8,128)(2,1)} async-done(((bf16[16,4,2,32,256]{4,3,2,1,0:T(8,128)(2,1)}), bf16[16,4,2,32,256]{4,3,2,1,0:T(8,128)(2,1)}, u32[]{:S(2)}, u32[]{:S(2)}) %all-to-all-start.6) | async-done | bytes 2097184 | tf_op jit(solution)/shard_map/all_to_all | solution.py:21
  130.3 8.2 %all_to_all.92 = bf16[2,64,2,32,256]{4,3,2,1,0:T(8,128)(2,1)} all-to-all(bf16[2,64,2,32,256]{4,3,2,1,0:T(8,128)(2,1)S(1)} %pad_maximum_fusion), channel_id=1, replica_groups=mesh['pb_0'=16,'pb_1'=4,'pb_2'=2,'vert'=4] {'pb_2'}, dimensions={0} | all-to-all | bytes 8388608 | tf_op jit(solution)/shard_map/all_to_all | solution.py:21
  139.2 13.0 %all-to-all-start.3 = ((bf16[64,2,2,256]{3,2,1,0:T(2,128)(2,1)}), bf16[64,2,2,256]{3,2,1,0:T(2,128)(2,1)S(1)}, u32[]{:S(2)}, u32[]{:S(2)}) async-start(bf16[64,2,2,256]{3,2,1,0:T(2,128)(2,1)} %broadcast_in_dim.48), calls=%async_computation.3 | async-start | bytes 262144 | tf_op jit(solution)/shard_map/all_to_all | solution.py:35
  154.8 4.3 copy.187
  160.4 8.6 %all-to-all-done.3 = bf16[64,2,2,256]{3,2,1,0:T(2,128)(2,1)S(1)} async-done(((bf16[64,2,2,256]{3,2,1,0:T(2,128)(2,1)}), bf16[64,2,2,256]{3,2,1,0:T(2,128)(2,1)S(1)}, u32[]{:S(2)}, u32[]{:S(2)}) %all-to-all-start.3) | async-done | bytes 131104 | tf_op jit(solution)/shard_map/all_to_all | solution.py:35
  169.8 3.4 all-to-all-start.8
  174.1 5.3 %all-to-all-done.8 = bf16[4,6,16,256]{3,2,1,0:T(8,128)(2,1)S(1)} async-done(((bf16[4,6,16,256]{3,2,1,0:T(8,128)(2,1)}), bf16[4,6,16,256]{3,2,1,0:T(8,128)(2,1)S(1)}, u32[]{:S(2)}, u32[]{:S(2)}) %all-to-all-start.8) | async-done | bytes 196640 | tf_op jit(solution)/shard_map/all_to_all | solution.py:35
  180.0 3.2 all-to-all-start.1
  184.8 42.9 %while.10 = (s32[]{:T(128)}, f32[3,256,256]{2,1,0:T(8,128)}, s32[3]{0:T(128)}, bf16[3,2,16,1024]{3,2,1,0:T(8,128)(2,1)}, s32[3]{0:T(128)}, /*index=5*/bf16[2,102...) while((s32[]{:T(128)}, f32[3,256,256]{2,1,0:T(8,128)}, ...), condition=%wide.region_4.5_spmd, body=%wide.region_3.4_spmd.sunk | while | flops 168534016 | bytes 3883733 | solution.py:136
  227.9 3.9 all_to_all.93
  231.9 3.1 broadcast_in_dim.52
  234.9 5.0 %all-to-all-start.9 = ((f32[4,3,256,256]{3,2,1,0:T(8,128)}), f32[4,3,256,256]{3,2,1,0:T(8,128)}, u32[]{:S(2)}, u32[]{:S(2)}) async-start(f32[4,3,256,256]{3,2,1,0:T(8,128)} %broadcast_in_dim.52), calls=%async_computation.9 | async-start | bytes 6291456 | tf_op jit(solution)/shard_map/all_to_all | solution.py:35
  242.3 35.7 %all-to-all-done.9 = f32[4,3,256,256]{3,2,1,0:T(8,128)} async-done(((f32[4,3,256,256]{3,2,1,0:T(8,128)}), f32[4,3,256,256]{3,2,1,0:T(8,128)}, u32[]{:S(2)}, u32[]{:S(2)}) %all-to-all-start.9) | async-done | bytes 3145760 | tf_op jit(solution)/shard_map/all_to_all | solution.py:35
  278.0 3.1 reduce_sum.93
  284.7 4.9 %all_to_all.94 = f32[2,64,2,2,256]{4,1,3,2,0:T(8,128)} all-to-all(f32[2,64,2,2,256]{4,1,3,2,0:T(8,128)S(1)} %convolution_bitcast_fusion.2), channel_id=1, replica_groups=mesh['pb_0'=16,'pb_1'=4,'pb_2'=2,'vert'=4] {'pb_2'}, dimensions={0} | all-to-all | bytes 1048576 | tf_op jit(solution)/shard_map/all_to_all | solution.py:61
  290.5 6.6 %all-to-all-start.2 = ((f32[64,2,1024]{2,1,0:T(2,128)}), f32[64,2,1024]{2,1,0:T(2,128)}, u32[]{:S(2)}, u32[]{:S(2)}) async-start(f32[64,2,1024]{2,1,0:T(2,128)} %broadcast_in_dim.44), calls=%async_computation.2 | async-start | bytes 1048576 | tf_op jit(solution)/shard_map/all_to_all | solution.py:35
  299.2 31.0 %all-to-all-done.2 = f32[64,2,1024]{2,1,0:T(2,128)} async-done(((f32[64,2,1024]{2,1,0:T(2,128)}), f32[64,2,1024]{2,1,0:T(2,128)}, u32[]{:S(2)}, u32[]{:S(2)}) %all-to-all-start.2) | async-done | bytes 524320 | tf_op jit(solution)/shard_map/all_to_all | solution.py:35
  330.2 5.9 %all-to-all-start.11 = ((f32[64,2,2,256]{3,2,1,0:T(2,128)}), f32[64,2,2,256]{3,2,1,0:T(2,128)S(1)}, u32[]{:S(2)}, u32[]{:S(2)}) async-start(f32[64,2,2,256]{3,2,1,0:T(2,128)} %copy.158), calls=%async_computation.11 | async-start | bytes 524288 | tf_op jit(solution)/shard_map/all_to_all | solution.py:69
  337.4 20.0 %all-to-all-done.11 = f32[64,2,2,256]{3,2,1,0:T(2,128)S(1)} async-done(((f32[64,2,2,256]{3,2,1,0:T(2,128)}), f32[64,2,2,256]{3,2,1,0:T(2,128)S(1)}, u32[]{:S(2)}, u32[]{:S(2)}) %all-to-all-start.11) | async-done | bytes 262176 | tf_op jit(solution)/shard_map/all_to_all | solution.py:69
  359.2 5.8 %all-to-all-start.14 = ((bf16[64,2,2,256]{3,2,1,0:T(2,128)(2,1)}), bf16[64,2,2,256]{3,2,1,0:T(2,128)(2,1)S(1)}, u32[]{:S(2)}, u32[]{:S(2)}) async-start(bf16[64,2,2,256]{3,2,1,0:T(2,128)(2,1)} %broadcast_in_dim.55), calls=%async_computation.14 | async-start | bytes 262144 | tf_op jit(solution)/shard_map/all_to_all | solution.py:35
  365.2 15.3 %all-to-all-done.14 = bf16[64,2,2,256]{3,2,1,0:T(2,128)(2,1)S(1)} async-done(((bf16[64,2,2,256]{3,2,1,0:T(2,128)(2,1)}), bf16[64,2,2,256]{3,2,1,0:T(2,128)(2,1)S(1)}, u32[]{:S(2)}, u32[]{:S(2)}) %all-to-all-start.14) | async-done | bytes 131104 | tf_op jit(solution)/shard_map/all_to_all | solution.py:35
  380.8 3.9 all_to_all.95
  390.7 4.9 %all_to_all.96 = f32[2,64,2,2,256]{4,1,3,2,0:T(8,128)} all-to-all(f32[2,64,2,2,256]{4,1,3,2,0:T(8,128)S(1)} %convolution_bitcast_fusion.1), channel_id=1, replica_groups=mesh['pb_0'=16,'pb_1'=4,'pb_2'=2,'vert'=4] {'pb_2'}, dimensions={0} | all-to-all | bytes 1048576 | tf_op jit(solution)/shard_map/all_to_all | solution.py:61
  396.2 3.2 all-to-all-start.12
  401.5 5.4 %all-to-all-start.17 = ((f32[64,2,2,256]{3,2,1,0:T(2,128)}), f32[64,2,2,256]{3,2,1,0:T(2,128)S(1)}, u32[]{:S(2)}, u32[]{:S(2)}) async-start(f32[64,2,2,256]{3,2,1,0:T(2,128)} %copy.169), calls=%async_computation.17 | async-start | bytes 524288 | tf_op jit(solution)/shard_map/all_to_all | solution.py:69
  406.9 22.5 %all-to-all-done.17 = f32[64,2,2,256]{3,2,1,0:T(2,128)S(1)} async-done(((f32[64,2,2,256]{3,2,1,0:T(2,128)}), f32[64,2,2,256]{3,2,1,0:T(2,128)S(1)}, u32[]{:S(2)}, u32[]{:S(2)}) %all-to-all-start.17) | async-done | bytes 262176 | tf_op jit(solution)/shard_map/all_to_all | solution.py:69
  430.3 6.2 %all-to-all-start.13 = ((f32[64,2,1024]{2,1,0:T(2,128)}), f32[64,2,1024]{2,1,0:T(2,128)}, u32[]{:S(2)}, u32[]{:S(2)}) async-start(f32[64,2,1024]{2,1,0:T(2,128)} %broadcast_in_dim.54), calls=%async_computation.13 | async-start | bytes 1048576 | tf_op jit(solution)/shard_map/all_to_all | solution.py:35
  437.3 31.4 %all-to-all-done.13 = f32[64,2,1024]{2,1,0:T(2,128)} async-done(((f32[64,2,1024]{2,1,0:T(2,128)}), f32[64,2,1024]{2,1,0:T(2,128)}, u32[]{:S(2)}, u32[]{:S(2)}) %all-to-all-start.13) | async-done | bytes 524320 | tf_op jit(solution)/shard_map/all_to_all | solution.py:35
  470.0 2.8 fusion.16
  (132 shorter events, 71.2 us)
Async XLA Ops:
  0.0 357.5 %copy-start = (bf16[1024,1024]{1,0:T(8,128)(2,1)S(1)}, bf16[1024,1024]{1,0:T(8,128)(2,1)}, u32[]{:S(2)}) copy-start(bf16[1024,1024]{1,0:T(8,128)(2,1)} %param.15) | copy-start | bytes 6291460
  24.5 13.7 %copy-start.10 = (s32[3]{0:T(128)S(1)}, s32[3]{0:T(128)}, u32[]{:S(2)}) copy-start(s32[3]{0:T(128)} %param.17) | copy-start | bytes 40
  24.5 13.7 %copy-start.12 = (s32[3]{0:T(128)S(1)}, s32[3]{0:T(128)}, u32[]{:S(2)}) copy-start(s32[3]{0:T(128)} %param.18) | copy-start | bytes 40
  24.5 13.9 %copy-start.4 = (f32[2,2,256]{2,1,0:T(2,128)S(1)}, f32[2,2,256]{2,1,0:T(2,128)}, u32[]{:S(2)}) copy-start(f32[2,2,256]{2,1,0:T(2,128)} %param.13) | copy-start | bytes 12292
  24.5 13.9 %copy-start.11 = (s32[256]{0:T(256)S(1)}, s32[256]{0:T(256)}, u32[]{:S(2)}) copy-start(s32[256]{0:T(256)} %param.19) | copy-start | bytes 3076
  24.5 103.2 %all-to-all-start.6 = ((bf16[16,4,2,32,256]{4,3,2,1,0:T(8,128)(2,1)}), bf16[16,4,2,32,256]{4,3,2,1,0:T(8,128)(2,1)}, u32[]{:S(2)}, u32[]{:S(2)}) async-start(bf16[16,4,2,32,256]{4,3,2,1,0:T(8,128)(2,1)} %stack.40), calls=%async_computation.6 | async-start | bytes 4194304 | tf_op jit(solution)/shard_map/all_to_all | solution.py:21
  38.4 134.7 %copy-start.2 = (bf16[2,2,256]{2,0,1:T(2,128)(2,1)}, bf16[2,2,256]{2,0,1:T(2,128)(2,1)S(1)}, u32[]{:S(2)}) copy-start(bf16[2,2,256]{2,0,1:T(2,128)(2,1)S(1)} %copy.196) | copy-start | bytes 6148
  38.6 120.5 %copy-start.6 = (s32[6]{0:T(128)}, s32[6]{0:T(128)S(1)}, u32[]{:S(2)}) copy-start(s32[6]{0:T(128)S(1)} %select_reduce_fusion) | copy-start | bytes 76
  139.2 29.9 %all-to-all-start.3 = ((bf16[64,2,2,256]{3,2,1,0:T(2,128)(2,1)}), bf16[64,2,2,256]{3,2,1,0:T(2,128)(2,1)S(1)}, u32[]{:S(2)}, u32[]{:S(2)}) async-start(bf16[64,2,2,256]{3,2,1,0:T(2,128)(2,1)} %broadcast_in_dim.48), calls=%async_computation.3 | async-start | bytes 262144 | tf_op jit(solution)/shard_map/all_to_all | solution.py:35
  169.8 9.7 %all-to-all-start.8 = ((bf16[4,6,16,256]{3,2,1,0:T(8,128)(2,1)}), bf16[4,6,16,256]{3,2,1,0:T(8,128)(2,1)S(1)}, u32[]{:S(2)}, u32[]{:S(2)}) async-start(bf16[4,6,16,256]{3,2,1,0:T(8,128)(2,1)} %broadcast_in_dim.51), calls=%async_computation.8 | async-start | bytes 393216 | tf_op jit(solution)/shard_map/all_to_all | solution.py:35
  180.0 47.7 %all-to-all-start.1 = ((f32[2,2,1024]{2,1,0:T(2,128)}), f32[2,2,1024]{2,1,0:T(2,128)S(1)}, u32[]{:S(2)}, u32[]{:S(2)}) async-start(f32[2,2,1024]{2,1,0:T(2,128)} %broadcast_in_dim.43), calls=%async_computation.1 | async-start | bytes 32768 | tf_op jit(solution)/shard_map/all_to_all | solution.py:35
  184.8 43.0 %copy-start.1 = (bf16[64,2,2,256]{3,2,0,1:T(2,128)(2,1)S(1)}, bf16[64,2,2,256]{3,2,0,1:T(2,128)(2,1)}, u32[]{:S(2)}) copy-start(bf16[64,2,2,256]{3,2,0,1:T(2,128)(2,1)} %copy.148) | copy-start | bytes 393220
  234.9 6.2 %copy-start.7 = (s32[6]{0:T(128)S(1)}, s32[6]{0:T(128)}, u32[]{:S(2)}) copy-start(s32[6]{0:T(128)} %copy-done.6) | copy-start | bytes 76
  234.9 43.0 %all-to-all-start.9 = ((f32[4,3,256,256]{3,2,1,0:T(8,128)}), f32[4,3,256,256]{3,2,1,0:T(8,128)}, u32[]{:S(2)}, u32[]{:S(2)}) async-start(f32[4,3,256,256]{3,2,1,0:T(8,128)} %broadcast_in_dim.52), calls=%async_computation.9 | async-start | bytes 6291456 | tf_op jit(solution)/shard_map/all_to_all | solution.py:35
  289.6 67.9 %copy-start.3 = (bf16[2,2,256]{2,0,1:T(2,128)(2,1)S(1)}, bf16[2,2,256]{2,0,1:T(2,128)(2,1)}, u32[]{:S(2)}) copy-start(bf16[2,2,256]{2,0,1:T(2,128)(2,1)} %copy-done.2) | copy-start | bytes 6148
  289.6 67.9 %copy-start.8 = (f32[2,256]{1,0:T(2,128)S(1)}, f32[2,256]{1,0:T(2,128)}, u32[]{:S(2)}) copy-start(f32[2,256]{1,0:T(2,128)} %param.12) | copy-start | bytes 6148
  290.5 39.7 %all-to-all-start.2 = ((f32[64,2,1024]{2,1,0:T(2,128)}), f32[64,2,1024]{2,1,0:T(2,128)}, u32[]{:S(2)}, u32[]{:S(2)}) async-start(f32[64,2,1024]{2,1,0:T(2,128)} %broadcast_in_dim.44), calls=%async_computation.2 | async-start | bytes 1048576 | tf_op jit(solution)/shard_map/all_to_all | solution.py:35
  330.2 27.1 %all-to-all-start.11 = ((f32[64,2,2,256]{3,2,1,0:T(2,128)}), f32[64,2,2,256]{3,2,1,0:T(2,128)S(1)}, u32[]{:S(2)}, u32[]{:S(2)}) async-start(f32[64,2,2,256]{3,2,1,0:T(2,128)} %copy.158), calls=%async_computation.11 | async-start | bytes 524288 | tf_op jit(solution)/shard_map/all_to_all | solution.py:69
  359.2 21.3 %all-to-all-start.14 = ((bf16[64,2,2,256]{3,2,1,0:T(2,128)(2,1)}), bf16[64,2,2,256]{3,2,1,0:T(2,128)(2,1)S(1)}, u32[]{:S(2)}, u32[]{:S(2)}) async-start(bf16[64,2,2,256]{3,2,1,0:T(2,128)(2,1)} %broadcast_in_dim.55), calls=%async_computation.14 | async-start | bytes 262144 | tf_op jit(solution)/shard_map/all_to_all | solution.py:35
  390.7 45.8 %copy-start.9 = (f32[3]{0:T(128)S(1)}, f32[3]{0:T(128)}, u32[]{:S(2)}) copy-start(f32[3]{0:T(128)} %param.16) | copy-start | bytes 40
  396.2 5.3 %all-to-all-start.12 = ((f32[2,2,1024]{2,1,0:T(2,128)}), f32[2,2,1024]{2,1,0:T(2,128)S(1)}, u32[]{:S(2)}, u32[]{:S(2)}) async-start(f32[2,2,1024]{2,1,0:T(2,128)} %broadcast_in_dim.53), calls=%async_computation.12 | async-start | bytes 32768 | tf_op jit(solution)/shard_map/all_to_all | solution.py:35
  399.4 70.5 %copy-start.5 = (f32[2,2,256]{2,1,0:T(2,128)S(1)}, f32[2,2,256]{2,1,0:T(2,128)}, u32[]{:S(2)}) copy-start(f32[2,2,256]{2,1,0:T(2,128)} %param.13) | copy-start | bytes 12292
  401.5 27.9 %all-to-all-start.17 = ((f32[64,2,2,256]{3,2,1,0:T(2,128)}), f32[64,2,2,256]{3,2,1,0:T(2,128)S(1)}, u32[]{:S(2)}, u32[]{:S(2)}) async-start(f32[64,2,2,256]{3,2,1,0:T(2,128)} %copy.169), calls=%async_computation.17 | async-start | bytes 524288 | tf_op jit(solution)/shard_map/all_to_all | solution.py:69
  430.3 38.4 %all-to-all-start.13 = ((f32[64,2,1024]{2,1,0:T(2,128)}), f32[64,2,1024]{2,1,0:T(2,128)}, u32[]{:S(2)}, u32[]{:S(2)}) async-start(f32[64,2,1024]{2,1,0:T(2,128)} %broadcast_in_dim.54), calls=%async_computation.13 | async-start | bytes 1048576 | tf_op jit(solution)/shard_map/all_to_all | solution.py:35
